TPU v7x, 128 devices: a whole 4x4x4 slice. The times are simulated.
128 devices in a mesh: node: 4 (over z), wide: 32 (over y, x, core).
Axes of the slice: x: 4, y: 4, z: 4, core: 2. Of those that a mesh axis runs over, the one named last changes fastest.
Arguments:
- tokens: bfloat16 [65536, 768], P(('node', 'wide')), may hold values from -6 to 6
- expert_index: int32 [65536, 1], P(('node', 'wide')), may hold values from 0 to 255; in each aligned block of 512 rows (0 to 511, 512 to 1023, ...) at most 4 rows name the same one
- norm_gain: float32 [768], replicated, may hold values from 0.5 to 1.5
- router_weight: float32 [768, 256], replicated, may hold values from -0.21875 to 0.21875
- expert_in: bfloat16 [256, 768, 3072], P(('node', 'wide')), may hold values from -0.21875 to 0.21875
- expert_out: bfloat16 [256, 3072, 768], P(('node', 'wide')), may hold values from -0.109375 to 0.109375
- post_gain: float32 [768], replicated, may hold values from 0.5 to 1.5
- dense_in: bfloat16 [3072, 768], P('node'), may hold values from -0.21875 to 0.21875
- scale_in: float32 [3072], P('node'), may hold values from 0.5 to 2
- dense_out: bfloat16 [3072, 768], P('node'), may hold values from -0.109375 to 0.109375
- scale_out: float32 [768], replicated, may hold values from 0.5 to 2
Outputs:
- layer_out: bfloat16 [65536, 768], P(('node', 'wide'))
Inputs may be any that keep to these rules, and one draw needn't show every extreme that they name: `expert_index`: in each aligned block of 512 rows (the tokens of one device) no expert is named by more than 4 rows, a bound that some block reaches.
All inputs are finite; a program needn't handle non-finite values.
Results may differ from a plain program's by a relative error of at most 0.01.
Values may be sent and summed in bfloat16 or wider, within the bound.
No kernel may reach another device: no remote copies, remote signals or barrier semaphores. Data moves between devices by JAX's collectives and lax.ppermute only.
A program may use at most 128 MiB of HBM per device.

v0:
```python
import jax
import jax.numpy as jnp
from jax import lax
from jax.sharding import PartitionSpec as P


def on_whole(share, axis, dim, apply):
    everything = lax.all_gather(share, axis, axis=dim, tiled=True)
    return apply(everything, jnp.int32(0))


def root_norm(values, gain_vector):
    floats = values.astype(jnp.float32)
    square_mean = jnp.mean(floats * floats, axis=-1, keepdims=True)
    return (floats * lax.rsqrt(square_mean + 1e-06) * gain_vector).astype(jnp.bfloat16)


def per_device(
    tokens,
    expert_index,
    norm_gain,
    router_weight,
    expert_in,
    expert_out,
    post_gain,
    dense_in,
    scale_in,
    dense_out,
    scale_out,
):
    tok_dev = tokens.shape[0]
    model_width = tokens.shape[1]
    experts = router_weight.shape[1]
    held_experts = expert_in.shape[0]
    devices = experts // held_experts
    capacity = max(2, 2 * tok_dev // experts)
    total_rows = experts * capacity
    normed = root_norm(tokens, norm_gain)
    chosen = expert_index[:, 0]
    columns = lax.broadcasted_iota(jnp.int32, (tok_dev, experts), 1)
    picked = chosen[:, None] == columns
    logits = jnp.dot(normed.astype(jnp.float32), router_weight, precision=lax.Precision.HIGHEST)
    picked_logit = jnp.sum(jnp.where(picked, logits, 0.0), axis=1)
    gate_prob = 1.0 / (1.0 + jnp.exp(-picked_logit))
    onehot = picked.astype(jnp.bfloat16)
    earlier = (
        lax.broadcasted_iota(jnp.int32, (tok_dev, tok_dev), 0)
        > lax.broadcasted_iota(jnp.int32, (tok_dev, tok_dev), 1)
    ).astype(jnp.bfloat16)
    before = jnp.dot(earlier, onehot, preferred_element_type=jnp.float32)
    slot_index = jnp.sum(jnp.where(picked, before, 0.0), axis=1).astype(jnp.int32)
    position = (
        chosen % held_experts * (devices * capacity)
        + chosen // held_experts * capacity
        + slot_index
    )
    dispatch = (
        lax.broadcasted_iota(jnp.int32, (total_rows, tok_dev), 0) == position[None, :]
    ).astype(jnp.bfloat16)
    outgoing = jnp.dot(dispatch, normed, preferred_element_type=jnp.float32).astype(jnp.bfloat16)
    packed = outgoing.reshape(held_experts, devices, capacity, model_width)
    arrived_rows = lax.all_to_all(packed, ("node", "wide"), split_axis=1, concat_axis=1, tiled=True)
    flat_rows = arrived_rows.reshape(held_experts, -1, model_width)
    apply_hidden = jnp.einsum(
        "jrd,jdf->jrf", flat_rows, expert_in, preferred_element_type=jnp.float32
    )
    apply_hidden = jax.nn.relu(apply_hidden).astype(jnp.bfloat16)
    produced = jnp.einsum(
        "jrf,jfd->jrd", apply_hidden, expert_out, preferred_element_type=jnp.float32
    )
    returned = lax.all_to_all(
        produced.astype(jnp.bfloat16).reshape(arrived_rows.shape),
        ("node", "wide"),
        split_axis=1,
        concat_axis=1,
        tiled=True,
    )
    expert_result = jnp.take(returned.reshape(total_rows, model_width), position, axis=0)
    residual = (
        tokens.astype(jnp.float32) + gate_prob[:, None] * expert_result.astype(jnp.float32)
    ).astype(jnp.bfloat16)
    normed2 = root_norm(residual, post_gain)

    def hidden_columns(pieces):
        codes_piece, scales_piece = pieces
        projected = lax.dot_general(
            normed2, codes_piece, (((1,), (1,)), ((), ())), preferred_element_type=jnp.float32
        )
        return jax.nn.relu(projected * scales_piece[None, :]).astype(jnp.bfloat16)

    hidden = on_whole(
        (dense_in, scale_in.astype(jnp.bfloat16)),
        "node",
        0,
        lambda piece, start: hidden_columns((piece[0], piece[1].astype(jnp.float32))),
    )
    dense_sum = jnp.dot(
        hidden,
        lax.all_gather(dense_out, "node", axis=0, tiled=True),
        preferred_element_type=jnp.float32,
    )
    return (residual.astype(jnp.float32) + dense_sum * scale_out[None, :]).astype(jnp.bfloat16)


def solution(mesh):
    return jax.shard_map(
        per_device,
        mesh=mesh,
        in_specs=(
            P(("node", "wide"), None),
            P(("node", "wide"), None),
            P(),
            P(),
            P(("node", "wide"), None, None),
            P(("node", "wide"), None, None),
            P(),
            P("node", None),
            P("node"),
            P("node", None),
            P(),
        ),
        out_specs=P(("node", "wide"), None),
        check_vma=False,
    )
```

profile of v0, /device:TPU:1, one launch (start us, length us, event | category | flops | bytes accessed | tf_op | source)
XLA Modules:
  0.0 170.1 jit_solution(11452180451006933273)
XLA Ops:
  6.5 0.7 all-gather.4.cloned.1.call-update
  7.3 0.0 all-gather.6.cloned.1.call-start
  7.3 0.7 all-gather.6.cloned.1.call-update
  8.0 0.4 fusion.11
  8.4 0.2 fusion.2
  8.7 2.4 %fusion.1 = bf16[1024,768]{1,0:T(8,128)(2,1)} fusion(s32[512]{0:T(512)S(1)} %fusion.25, bf16[512,768]{1,0:T(8,128)(2,1)S(1)} %copy-done.1, f32[768]{0:T(1024)S(1)} %copy-done.4, f32[512]{0:T(512)S(1)} %add_rsqrt_fusion.1), kind=kOutput, calls=%fused_computation.11 | convolution fusion | flops 808189952 | bytes 2366464 | tf_op jit(solution)/shard_map/dot_general | solution.py:60
  11.0 2.9 %reshape.106 = bf16[2,128,4,768]{3,2,1,0:T(4,128)(2,1)S(1)} reshape(bf16[1024,768]{1,0:T(8,128)(2,1)} %fusion.1) | data formatting | bytes 3145728 | tf_op jit(solution)/shard_map/reshape | solution.py:61
  13.9 0.5 copy.15
  14.5 36.1 %all_to_all.10 = bf16[2,128,4,768]{3,2,0,1:T(4,128)(2,1)S(1)} all-to-all(bf16[2,128,4,768]{3,2,0,1:T(4,128)(2,1)S(1)} %copy.15), channel_id=1, replica_groups=mesh['node'=4,'wide'=32] {'node','wide'}, dimensions={1} | all-to-all | bytes 3145728 | tf_op jit(solution)/shard_map/all_to_all | solution.py:62
  50.6 1.2 copy.16
  51.9 9.3 %maximum_convert_fusion = bf16[2,512,3072]{2,1,0:T(8,128)(2,1)S(1)} fusion(bf16[2,768,3072]{2,1,0:T(8,128)(2,1)} %param.15, bf16[2,512,768]{2,0,1:T(2,128)(2,1)S(1)} %bitcast.11), kind=kOutput, calls=%fused_computation.1 | convolution fusion | flops 4838129664 | bytes 17301504 | tf_op jit(solution)/shard_map/jrd,jdf->jrf/dot_general | solution.py:64
  61.2 6.2 %convolution_convert_fusion = bf16[2,512,768]{2,1,0:T(8,128)(2,1)} fusion(bf16[2,512,3072]{2,1,0:T(8,128)(2,1)S(1)} %maximum_convert_fusion, bf16[2,3072,768]{2,1,0:T(8,128)(2,1)S(1)} %bitcast.19), kind=kOutput, calls=%fused_computation.12 | convolution fusion | flops 4832624640 | bytes 17301504 | tf_op jit(solution)/shard_map/jrf,jfd->jrd/dot_general | solution.py:68
  67.4 2.9 %reshape.108 = bf16[2,128,4,768]{3,2,1,0:T(4,128)(2,1)S(1)} reshape(bf16[2,512,768]{2,1,0:T(8,128)(2,1)} %convolution_convert_fusion) | data formatting | bytes 3145728 | tf_op jit(solution)/shard_map/reshape | solution.py:72
  70.3 1.7 %copy.18 = bf16[2,128,4,768]{3,2,0,1:T(4,128)(2,1)} copy(bf16[2,128,4,768]{3,2,1,0:T(4,128)(2,1)S(1)} %reshape.108) | data formatting | bytes 3145728 | tf_op jit(solution)/shard_map/reshape | solution.py:72
  72.0 4.5 %all-to-all-start.1 = ((bf16[2,128,4,768]{3,2,0,1:T(4,128)(2,1)}), bf16[2,128,4,768]{3,2,0,1:T(4,128)(2,1)S(1)}, u32[]{:S(2)}, u32[]{:S(2)}) async-start(bf16[2,128,4,768]{3,2,0,1:T(4,128)(2,1)} %copy.18), calls=%async_computation.1 | async-start | bytes 3145728 | tf_op jit(solution)/shard_map/all_to_all | solution.py:71
  76.6 19.1 %all-gather = bf16[4,1,768]{2,1,0:T(2,128)(2,1)S(1)} all-gather(bf16[1,1,768]{2,1,0:T(2,128)(2,1)S(1)} %reshape.118), channel_id=1, replica_groups=mesh['node'=4,'wide'=32] {'node'}, dimensions={0}, use_global_device_ids=true | all-gather | bytes 7680 | tf_op jit(solution)/shard_map/all_gather | solution.py:8
  95.8 1.0 fusion.12
  96.8 4.7 %all-to-all-done.1 = bf16[2,128,4,768]{3,2,0,1:T(4,128)(2,1)S(1)} async-done(((bf16[2,128,4,768]{3,2,0,1:T(4,128)(2,1)}), bf16[2,128,4,768]{3,2,0,1:T(4,128)(2,1)S(1)}, u32[]{:S(2)}, u32[]{:S(2)}) %all-to-all-start.1) | async-done | bytes 1572896 | tf_op jit(solution)/shard_map/all_to_all | solution.py:71
  101.5 1.7 %copy.19 = bf16[2,128,4,768]{3,2,1,0:T(4,128)(2,1)} copy(bf16[2,128,4,768]{3,2,0,1:T(4,128)(2,1)S(1)} %all-to-all-done.1) | data formatting | bytes 3145728 | tf_op jit(solution)/shard_map/all_to_all | solution.py:71
  103.2 2.7 %reshape.109 = bf16[1024,768]{1,0:T(8,128)(2,1)S(1)} reshape(bf16[2,128,4,768]{3,2,1,0:T(4,128)(2,1)} %copy.19) | data formatting | bytes 3145728 | tf_op jit(solution)/shard_map/reshape | solution.py:78
  106.0 2.7 %gather_fusion = bf16[512,768]{1,0:T(8,128)(2,1)} fusion(bf16[1024,768]{1,0:T(8,128)(2,1)S(1)} %reshape.109, s32[1024]{0:T(1024)S(1)} %pad_clamp_fusion), kind=kCustom, calls=%fused_computation | custom fusion | bytes 1574912 | tf_op jit(solution)/shard_map/jit(_take)/gather | solution.py:78
  108.7 1.8 %fusion.6 = (f32[512]{0:T(512)S(1)}, bf16[512,768]{1,0:T(8,128)(2,1)S(1)}) fusion(bf16[512,768]{1,0:T(8,128)(2,1)} %gather_fusion, pred[512]{0:T(512)(128)(4,1)S(1)} %get-tuple-element.7, f32[512]{0:T(512)S(1)} %add_divide_fusion, bf16[512,768]{1,0:T(8,128)(2,1)S(1)} %copy-done.1), kind=kLoop, calls=%fused_computation.17 | loop fusion | flops 3538432 | bytes 2363904 | tf_op jit(solution)/shard_map/reduce_sum | solution.py:14
  110.6 42.7 %all-gather.6.cloned.1.call-done = bf16[3072,768]{1,0:T(8,128)(2,1)} async-done(((bf16[768,768]{1,0:T(8,128)(2,1)}), bf16[3072,768]{1,0:T(8,128)(2,1)}) %all-gather.6.cloned.1.call-update) | async-done | bytes 4718608 | tf_op jit(solution)/shard_map/all_gather | solution.py:99
  153.3 9.9 %fusion.9 = bf16[512,768]{1,0:T(8,128)(2,1)} fusion(bf16[512,768]{1,0:T(8,128)(2,1)S(1)} %get-tuple-element.6, bf16[3072,768]{1,0:T(8,128)(2,1)} %all-gather.6.cloned.1.call-done, bf16[3072,768]{1,0:T(8,128)(2,1)} %all-gather.4.cloned.1.call-done, f32[3072]{0:T(1024)S(1)} %bitcast.12, f32[768]{0:T(1024)S(1)} %copy-done.5, f32[768]{0:T(1024)S(1)} %copy-done.6, ...), kind=kOutput, calls=%fused_computation.20 | convolution fusion | flops 4839702528 | bytes 11030528 | tf_op jit(solution)/shard_map/dot_general | solution.py:97
  (33 shorter events, 0.2 us)
Async XLA Ops:
  6.5 89.2 %copy-start = (f32[768,256]{1,0:T(8,128)S(1)}, f32[768,256]{1,0:T(8,128)}, u32[]{:S(2)}) copy-start(f32[768,256]{1,0:T(8,128)} %param.14) | copy-start | bytes 2359300
  6.5 1.5 copy-start.2
  6.5 1.9 %copy-start.1 = (bf16[512,768]{1,0:T(8,128)(2,1)S(1)}, bf16[512,768]{1,0:T(8,128)(2,1)}, u32[]{:S(2)}) copy-start(bf16[512,768]{1,0:T(8,128)(2,1)} %param.11) | copy-start | bytes 2359300
  6.5 104.0 %all-gather.4.cloned.1.call-start = ((), (), s32[]{:S(2)}) async-start(), calls=%async_computation.2 | async-start | bytes 5898240 | tf_op jit(solution)/shard_map/all_gather | solution.py:8
  7.3 1.4 copy-start.4
  7.3 146.0 %all-gather.6.cloned.1.call-start = ((), (), s32[]{:S(2)}) async-start(), calls=%async_computation.3 | async-start | bytes 5898240 | tf_op jit(solution)/shard_map/all_gather | solution.py:99
  50.6 10.6 %slice-start = ((s8[9437184]{0:T(1024)(128)(4,1)}), s8[4194304]{0:T(1024)(128)(4,1)S(1)}, s32[]{:S(2)}) async-start(s8[9437184]{0:T(1024)(128)(4,1)} %bitcast.18), calls=%async_computation.4 | async-start | bytes 8388608
  51.9 9.3 %slice-start.1 = ((s8[9437184]{0:T(1024)(128)(4,1)}), s8[4194304]{0:T(1024)(128)(4,1)S(1)}, s32[]{:S(2)}) async-start(s8[9437184]{0:T(1024)(128)(4,1)} %bitcast.18), calls=%async_computation.5 | async-start | bytes 8388608
  51.9 9.3 %slice-start.2 = ((s8[9437184]{0:T(1024)(128)(4,1)}), s8[1048576]{0:T(1024)(128)(4,1)S(1)}, s32[]{:S(2)}) async-start(s8[9437184]{0:T(1024)(128)(4,1)} %bitcast.18), calls=%async_computation.6 | async-start | bytes 2097152
  72.0 4.5 %copy-start.3 = (f32[768]{0:T(1024)S(1)}, f32[768]{0:T(1024)}, u32[]{:S(2)}) copy-start(f32[768]{0:T(1024)} %param.19) | copy-start | bytes 9220
  72.0 29.5 %all-to-all-start.1 = ((bf16[2,128,4,768]{3,2,0,1:T(4,128)(2,1)}), bf16[2,128,4,768]{3,2,0,1:T(4,128)(2,1)S(1)}, u32[]{:S(2)}, u32[]{:S(2)}) async-start(bf16[2,128,4,768]{3,2,0,1:T(4,128)(2,1)} %copy.18), calls=%async_computation.1 | async-start | bytes 3145728 | tf_op jit(solution)/shard_map/all_to_all | solution.py:71
  108.7 44.6 %copy-start.5 = (f32[768]{0:T(1024)S(1)}, f32[768]{0:T(1024)}, u32[]{:S(2)}) copy-start(f32[768]{0:T(1024)} %param.21) | copy-start | bytes 9220
  108.7 44.6 %copy-start.6 = (f32[768]{0:T(1024)S(1)}, f32[768]{0:T(1024)}, u32[]{:S(2)}) copy-start(f32[768]{0:T(1024)} %param.17) | copy-start | bytes 9220
Sparse Core Ops, SparseCore 0:
  9.0 84.7 all-gather.3
  95.5 57.8 all-gather.5
where the time goes:
time: 171 us; the launch traced here: 170 us
  blocking collectives  55.2 us (32%)
  waiting for transfers between devices  48.9 us (29%)
  matrix products  29.1 us (17%)
  local copies, waits for them, and re-layouts  16.5 us (10%)
  between operations  13.6 us (8%)
  starting transfers between devices  4.57 us (3%)
  other arithmetic  2.15 us (1%)
    all_gather x1, waiting for transfers between devices, per_device(): lax.all_gather(dense_out, 'node', axis=0, tiled=True)  42.7 us
    all_to_all x1, blocking collectives, per_device(): lax.all_to_all(packed, ('node', 'wide'), split_axis=1, concat_axis=1, til...  36.1 us
    all_gather x1, blocking collectives, on_whole(): everything = lax.all_gather(share, axis, axis=dim, tiled=True)  19.1 us
    dot_general x1, matrix products, per_device(): jnp.dot(hidden, lax.all_gather(dense_out, 'node', axis=0, tiled=True), pr...  9.92 us
    dot_general x1, matrix products, per_device(): jnp.einsum('jrd,jdf->jrf', flat_rows, expert_in, preferred_element_type=j...  9.3 us
    dot_general x1, matrix products, per_device(): jnp.einsum('jrf,jfd->jrd', apply_hidden, expert_out, preferred_element_ty...  6.17 us
    all_to_all x1, waiting for transfers between devices, per_device(): lax.all_to_all(produced.astype(jnp.bfloat16).reshape(arrived_rows.shape),...  4.73 us
    reshape x2, local copies, waits for them, and re-layouts, per_device(): produced.astype(jnp.bfloat16).reshape(arrived_rows.shape)  4.6 us
  transfers between devices with their start and end apart: 3, of which 2 were waited for; matrix products, arithmetic and copies ran while one was open for 22% of the time, Pallas kernels for 0%

commit v1 on v0

v1 whole, which is shorter than its diff:
```python
import functools

import jax
import jax.numpy as jnp
from jax import lax
from jax.experimental import pallas as pl
from jax.experimental.pallas import tpu as pltpu
from jax.sharding import PartitionSpec as P

AXES = ("node", "wide")
Y_CHIPS, X_CHIPS, CORES = 4, 4, 2
COLORS = 4
FAR = 3
SCALE_ROWS = 8
LANES = 128
SUB = 8
BF16 = jnp.bfloat16
F32 = jnp.float32


def moved(value, nodes, dz=0, dy=0, dx=0, dc=0):
    def place(z, y, x, c):
        return ((z * Y_CHIPS + y) * X_CHIPS + x) * CORES + c

    pairs = [
        (
            place(z, y, x, c),
            place((z + dz) % nodes, (y + dy) % Y_CHIPS, (x + dx) % X_CHIPS, (c + dc) % CORES),
        )
        for z in range(nodes)
        for y in range(Y_CHIPS)
        for x in range(X_CHIPS)
        for c in range(CORES)
    ]
    return lax.ppermute(value, AXES, pairs)


def position():
    wide = lax.axis_index("wide")
    core = wide % CORES
    x_chip = (wide // CORES) % X_CHIPS
    y_chip = wide // (CORES * X_CHIPS)
    return core, ((x_chip + 2 * y_chip) % COLORS, (2 * x_chip + y_chip) % COLORS)


def joined(first, second):
    top = lax.broadcasted_iota(jnp.int32, first.shape, 1) < SUB // 2
    even = jnp.where(top, first, pltpu.roll(second, SUB // 2, 1))
    odd = jnp.where(top, pltpu.roll(first, SUB // 2, 1), second)
    return even, odd


def pack_columns(rows, block, out_ref):
    count = rows.shape[0] // SUB
    first = rows[:, :LANES].reshape(count, SUB, LANES)
    second = rows[:, LANES:].reshape(count, SUB, LANES)
    even, odd = joined(first, second)
    out_ref[:, 0, block * SUB : (block + 1) * SUB, :] = even.astype(out_ref.dtype)
    out_ref[:, 1, block * SUB : (block + 1) * SUB, :] = odd.astype(out_ref.dtype)


def unpack_messages(message_ref, held, rows_ref):
    count = message_ref.shape[0]
    blocks = rows_ref.shape[1] // (2 * LANES)
    for block in range(blocks):
        tile = slice((held * blocks + block) * SUB, (held * blocks + block + 1) * SUB)
        even = message_ref[:, 0, tile, :].astype(F32)
        odd = message_ref[:, 1, tile, :].astype(F32)
        first, second = joined(even, odd)
        start = block * 2 * LANES
        rows_ref[:, start : start + LANES] = first.reshape(count * SUB, LANES).astype(BF16)
        rows_ref[:, start + LANES : start + 2 * LANES] = second.reshape(count * SUB, LANES).astype(BF16)


def both_ways(row):
    count = row.shape[1]
    floats = row.astype(F32)
    turned = jnp.broadcast_to(floats, (LANES, count)).T
    along_rows = jnp.concatenate([turned] * (count // LANES), axis=1)
    return jnp.broadcast_to(floats, (count, count)), along_rows


def normed_rows(floats, gain):
    square_mean = jnp.mean(floats * floats, axis=-1, keepdims=True)
    return (floats * lax.rsqrt(square_mean + 1e-06) * gain).astype(BF16)


def cut_kernel(size, in_hbm, out_hbm, scale_ref, cut_ref, sems):
    half = in_hbm.shape[0] // 2
    core, colors = position()
    copies = []
    for part in range(2):
        start = pl.multiple_of(part * half + (colors[part] * CORES + core) * size, 16)
        for which, codes in enumerate((in_hbm, out_hbm)):
            copies.append(
                pltpu.make_async_copy(
                    codes.at[pl.ds(start, size), :],
                    cut_ref.at[pl.ds((part * 2 + which) * size, size), :],
                    sems.at[part * 2 + which],
                )
            )
    for copy in copies:
        copy.start()
    scale = scale_ref[...].reshape(1, -1)
    high = scale.astype(BF16).astype(F32)
    middle = (scale - high).astype(BF16).astype(F32)
    low = scale - high - middle
    lines = lax.broadcasted_iota(jnp.int32, (SCALE_ROWS, scale.shape[1]), 0)
    terms = jnp.where(lines == 0, high, jnp.where(lines == 1, middle, jnp.where(lines == 2, low, 0.0)))
    cut_ref[4 * size :, :] = terms.astype(BF16)
    for copy in copies:
        copy.wait()


def relay_kernel(size, *refs):
    far, (own, right, left, up, down, scales_ref, sems) = refs[:FAR], refs[FAR:]
    copies = []

    def copy(source, start, out, target):
        copies.append(
            pltpu.make_async_copy(
                source.at[pl.ds(start, size), :],
                out.at[pl.ds(target * size, size), :],
                sems.at[len(copies)],
            )
        )

    for index, source in enumerate(far):
        for part in range(2):
            whole, shared = ((right, left), (up, down))[part], ((up, down), (right, left))[part]
            for which in range(2):
                start = (part * 2 + which) * size
                copy(source, start, own, (index * 2 + part) * 2 + which)
                for out in whole:
                    copy(source, start, out, index * 2 + which)
                copy(source, start, shared[which], 2 * FAR + index)
    for one in copies:
        one.start()
    for index, source in enumerate(far):
        terms = source[4 * size :, :].astype(F32)
        scales_ref[index] = terms[0:1] + terms[1:2] + terms[2:3]
    for one in copies:
        one.wait()


def weave_copies(size, own_in, own_out, arrays, w_in, w_out, sems):
    shard = own_in.shape[0]
    core, colors = position()
    weights = (w_in, w_out)
    copies = [[[] for _ in range(FAR + 1)] for _ in range(2)]
    for which, own in enumerate((own_in, own_out)):
        copies[which][0].append(
            pltpu.make_async_copy(own, weights[which].at[pl.ds(0, shard), :], sems.at[which, 0])
        )

    def copy(array, row, index, part, which, color, swapped):
        line = (colors[part] + color) % COLORS
        line = line * CORES + (core + swapped) % CORES
        start = pl.multiple_of(shard * (index + 1) + part * (shard // 2) + line * size, 16)
        copies[which][index + 1].append(
            pltpu.make_async_copy(
                arrays[array].at[pl.ds(row * size, size), :],
                weights[which].at[pl.ds(start, size), :],
                sems.at[which, index + 1],
            )
        )

    for swapped in range(CORES):
        base = swapped * 5
        for index in range(FAR):
            for which in range(2):
                for part in range(2):
                    copy(base, (index * 2 + part) * 2 + which, index, part, which, 0, swapped)
                for side in range(4):
                    part, color = side // 2, (-1, 1)[side % 2]
                    copy(base + 1 + side, index * 2 + which, index, part, which, color, swapped)
                    if which == side % 2:
                        copy(base + 1 + side, 2 * FAR + index, index, 1 - part, which, 2, swapped)
    return copies


def dispatch_kernel(capacity, token_ref, row_ref, gain_ref, out_ref):
    normed = normed_rows(token_ref[...].astype(F32), gain_ref[...].reshape(1, -1))
    count = token_ref.shape[0]
    row = row_ref[...]
    along, across = both_ways(row)
    source = lax.broadcasted_iota(jnp.int32, (count, count), 0)
    target = lax.broadcasted_iota(jnp.int32, (count, count), 1)
    same = jnp.where((along == across) & (source < target), 1.0, 0.0)
    slot = jnp.sum(same, axis=0, keepdims=True).astype(jnp.int32)
    place = (row >> 1) * capacity + slot
    blocks = normed.shape[1] // (2 * LANES)
    for held in range(2):
        wanted = jnp.where((row & 1) == held, place, -1)
        selected = jnp.where(source == wanted, 1.0, 0.0).astype(BF16)
        for block in range(blocks):
            columns = normed[:, block * 2 * LANES : (block + 1) * 2 * LANES]
            rows = jnp.dot(selected, columns, preferred_element_type=F32)
            pack_columns(rows, held * blocks + block, out_ref)


def side_kernel(capacity, token_ref, row_ref, gain_ref, router_ref, gate_ref, place_ref):
    normed = normed_rows(token_ref[...].astype(F32), gain_ref[...].reshape(1, -1)).astype(F32)
    count = token_ref.shape[0]
    along, across = both_ways(row_ref[...])
    logits = jnp.dot(normed, router_ref[...], precision=lax.Precision.HIGHEST, preferred_element_type=F32)
    experts = logits.shape[1]
    columns = lax.broadcasted_iota(jnp.int32, (count, experts), 1).astype(F32)
    picked = jnp.sum(jnp.where(across[:, :experts] == columns, logits, 0.0), axis=1, keepdims=True)
    gate_ref[...] = 1.0 / (1.0 + jnp.exp(-picked))
    rank = lax.broadcasted_iota(jnp.int32, (count, count), 0)
    other = lax.broadcasted_iota(jnp.int32, (count, count), 1)
    same = jnp.where((along == across) & (other < rank), 1.0, 0.0)
    slot = jnp.sum(same, axis=1, keepdims=True).astype(jnp.int32)
    chosen = across[:, :1].astype(jnp.int32)
    place = (chosen >> 1) * capacity + slot
    for held in range(2):
        place_ref[:, held : held + 1] = jnp.where((chosen & 1) == held, place, -1)


def expert_kernel(message_ref, in_hbm, out_hbm, result_ref, rows, hidden, w_in, w_out, sems):
    held_experts, width, units = in_hbm.shape
    tile, parts = 512, 4
    copies = []
    for held in range(held_experts):
        for codes, weights in ((in_hbm, w_in), (out_hbm, w_out)):
            depth = codes.shape[1] // parts
            for part in range(parts):
                lines = pl.ds(part * depth, depth)
                copies.append(
                    pltpu.make_async_copy(
                        codes.at[held, lines, :], weights.at[held, lines, :], sems.at[len(copies)]
                    )
                )
    for copy in copies:
        copy.start()
    blocks = width // (2 * LANES)
    for held in range(held_experts):
        unpack_messages(message_ref, held, rows)
        first = held * 2 * parts
        for copy in copies[first : first + parts]:
            copy.wait()
        for step in range(units // tile):
            columns = slice(step * tile, (step + 1) * tile)
            value = jnp.dot(rows[...], w_in[held, :, columns], preferred_element_type=F32)
            hidden[:, columns] = jnp.maximum(value, 0.0).astype(BF16)
        for copy in copies[first + parts : first + 2 * parts]:
            copy.wait()
        for block in range(blocks):
            columns = slice(block * 2 * LANES, (block + 1) * 2 * LANES)
            value = jnp.dot(hidden[...], w_out[held, :, columns], preferred_element_type=F32)
            pack_columns(value, held * blocks + block, result_ref)


def tail_kernel(
    size,
    token_ref,
    gate_ref,
    place_ref,
    gain_ref,
    scale_ref,
    scale_out_ref,
    far_scale_ref,
    message_ref,
    own_in,
    own_out,
    *refs,
):
    arrays, (result_ref, w_in, w_out, rows, normed2, hidden, total, sems) = refs[:-8], refs[-8:]
    copies = weave_copies(size, own_in, own_out, arrays, w_in, w_out, sems)
    for side in copies:
        for node in side:
            for copy in node:
                copy.start()
    count, width = token_ref.shape
    slots = lax.broadcasted_iota(jnp.int32, (count, count), 1)
    for held in range(2):
        unpack_messages(message_ref, held, rows)
        picked = jnp.where(slots == place_ref[:, held : held + 1], 1.0, 0.0).astype(BF16)
        value = jnp.dot(picked, rows[...], preferred_element_type=F32)
        total[...] = value if held == 0 else total[...] + value
    residual = (token_ref[...].astype(F32) + gate_ref[...] * total[...]).astype(BF16)
    rows[...] = residual
    normed2[...] = normed_rows(residual.astype(F32), gain_ref[...].reshape(1, -1))

    tile = 256
    units = hidden.shape[1]
    shard = own_in.shape[0]
    own_scale = scale_ref[...].reshape(1, -1)
    for step in range(units // tile):
        block, inner = divmod(step * tile, shard)
        if inner == 0:
            for copy in copies[0][block]:
                copy.wait()
        scale = own_scale if block == 0 else far_scale_ref[block - 1]
        value = lax.dot_general(
            normed2[...],
            w_in[step * tile : (step + 1) * tile, :],
            (((1,), (1,)), ((), ())),
            preferred_element_type=F32,
        )
        value = jnp.maximum(value * scale[:, inner : inner + tile], 0.0)
        hidden[:, step * tile : (step + 1) * tile] = value.astype(BF16)
    for node in copies[1]:
        for copy in node:
            copy.wait()
    scale_out = scale_out_ref[...].reshape(1, -1)
    for step in range(width // tile):
        columns = slice(step * tile, (step + 1) * tile)
        value = jnp.dot(hidden[...], w_out[:, columns], preferred_element_type=F32)
        value = rows[:, columns].astype(F32) + value * scale_out[:, columns]
        result_ref[:, columns] = value.astype(BF16)


def vmem():
    return pl.BlockSpec(memory_space=pltpu.VMEM)


def hbm():
    return pl.BlockSpec(memory_space=pltpu.HBM)


def call(kernel, out_shape, in_specs, scratch=(), grant=16, flops=0, moved_bytes=0):
    return pl.pallas_call(
        kernel,
        out_shape=out_shape,
        in_specs=in_specs,
        out_specs=jax.tree.map(lambda _: vmem(), out_shape),
        scratch_shapes=list(scratch),
        compiler_params=pltpu.CompilerParams(vmem_limit_bytes=grant << 20),
        cost_estimate=pl.CostEstimate(
            flops=int(flops), bytes_accessed=int(moved_bytes), transcendentals=0
        ),
    )


def per_device(
    tokens,
    expert_index,
    norm_gain,
    router_weight,
    expert_in,
    expert_out,
    post_gain,
    dense_in,
    scale_in,
    dense_out,
    scale_out,
):
    tok_dev, width = tokens.shape
    experts = router_weight.shape[1]
    held_experts, _, units = expert_in.shape
    devices = experts // held_experts
    capacity = max(2, 2 * tok_dev // experts)
    shard = dense_in.shape[0]
    nodes = units // shard
    size = shard // 2 // (COLORS * CORES)
    message = (devices // 2, 2, held_experts * capacity * width // LANES, LANES)
    like = jax.ShapeDtypeStruct

    row = expert_index.reshape(1, tok_dev)
    dma = pltpu.SemaphoreType.DMA

    cut = call(
        functools.partial(cut_kernel, size),
        like((4 * size + SCALE_ROWS, width), BF16),
        [hbm(), hbm(), vmem()],
        [dma((4,))],
        grant=60,
        moved_bytes=6e5,
    )(dense_in, dense_out, scale_in)
    far = []
    for step in (1, -1, 2):
        far.append(moved(cut, nodes, dz=step))

    sent = call(
        functools.partial(dispatch_kernel, capacity),
        like(message, BF16),
        [vmem()] * 3,
        flops=4 * tok_dev * tok_dev * width,
        moved_bytes=4e6,
    )(tokens, row, norm_gain)

    def exchanged(value):
        flat = value.reshape((devices,) + message[2:])
        return lax.all_to_all(flat, AXES, split_axis=0, concat_axis=0, tiled=True).reshape(message)

    arrived = exchanged(sent)

    gate, places = call(
        functools.partial(side_kernel, capacity),
        [like((tok_dev, 1), F32), like((tok_dev, 2), jnp.int32)],
        [vmem()] * 4,
        flops=12 * tok_dev * experts * width,
        moved_bytes=4e6,
    )(tokens, row, norm_gain, router_weight)

    side = like((3 * FAR * size, width), BF16)
    own, right, left, up, down, far_scales = call(
        functools.partial(relay_kernel, size),
        [like((4 * FAR * size, width), BF16)] + [side] * 4 + [like((FAR, 1, shard), F32)],
        [vmem()] * FAR,
        [dma((16 * FAR,))],
        moved_bytes=6e6,
    )(*far)
    near = []
    for value, shift in ((right, {"dx": 1}), (left, {"dx": -1}), (up, {"dy": 1}), (down, {"dy": -1})):
        near.append(moved(value, nodes, **shift))
    pieces = [own] + near
    swapped = []
    for value in pieces:
        swapped.append(moved(value, nodes, dc=1))

    rows = devices * capacity
    produced = call(
        expert_kernel,
        like(message, BF16),
        [vmem(), hbm(), hbm()],
        [
            pltpu.VMEM((rows, width), BF16),
            pltpu.VMEM((rows, units), BF16),
            pltpu.VMEM((held_experts, width, units), BF16),
            pltpu.VMEM((held_experts, units, width), BF16),
            dma((8 * held_experts,)),
        ],
        grant=56,
        flops=4 * held_experts * rows * units * width,
        moved_bytes=2e7,
    )(arrived, expert_in, expert_out)
    returned = exchanged(produced)

    return call(
        functools.partial(tail_kernel, size),
        like(tokens.shape, BF16),
        [vmem()] * 8 + [hbm()] * 12,
        [
            pltpu.VMEM((units, width), BF16),
            pltpu.VMEM((units, width), BF16),
            pltpu.VMEM((tok_dev, width), BF16),
            pltpu.VMEM((tok_dev, width), BF16),
            pltpu.VMEM((tok_dev, units), BF16),
            pltpu.VMEM((tok_dev, width), F32),
            dma((2, FAR + 1)),
        ],
        grant=58,
        flops=4 * tok_dev * units * width,
        moved_bytes=1.2e7,
    )(
        tokens,
        gate,
        places,
        post_gain,
        scale_in,
        scale_out,
        far_scales,
        returned,
        dense_in,
        dense_out,
        *pieces,
        *swapped,
    )


def solution(mesh):
    return jax.shard_map(
        per_device,
        mesh=mesh,
        in_specs=(
            P(("node", "wide"), None),
            P(("node", "wide"), None),
            P(),
            P(),
            P(("node", "wide"), None, None),
            P(("node", "wide"), None, None),
            P(),
            P("node", None),
            P("node"),
            P("node", None),
            P(),
        ),
        out_specs=P(("node", "wide"), None),
        check_vma=False,
    )
```

time: 171 us -> 124 us (0.73)
  blocking collectives: 55.2 us -> 0 us
  Pallas kernels: 0 us -> 43.1 us
  starting transfers between devices: 4.57 us -> 34.5 us
  matrix products: 29.1 us -> 0 us
  between operations: 13.6 us -> 0.41 us
  waiting for transfers between devices: 48.9 us -> 38 us
  local copies, waits for them, and re-layouts: 16.5 us -> 7.11 us
  other arithmetic: 2.15 us -> 0 us
    pallas_call x0 -> x6, Pallas kernels: none -> 43.1 us  [the longest x1 19 us: per_device(): call(expert_kernel, like(message, BF16), [vmem(), hbm(), hbm()], [pltpu.V...]
    all_gather x2 -> x0, waiting for transfers between devices: 42.8 us -> none  [the longest x1 42.7 us: per_device(): lax.all_gather(dense_out, 'node', axis=0, tiled=True)]
    all_to_all x1 -> x0, blocking collectives: 36.1 us -> none  [per_device(): lax.all_to_all(packed, ('node', 'wide'), split_axis=1, concat_axis=1, til...]
    dot_general x6 -> x0, matrix products: 29.1 us -> none  [the longest x1 9.92 us: per_device(): jnp.dot(hidden, lax.all_gather(dense_out, 'node', axis=0, tiled=True), pr...]
    ppermute x0 -> x12, waiting for transfers between devices: none -> 20.4 us  [moved(): return lax.ppermute(value, AXES, pairs)]
    all_gather x1 -> x0, blocking collectives: 19.1 us -> none  [on_whole(): everything = lax.all_gather(share, axis, axis=dim, tiled=True)]
    all_to_all x1 -> x2, starting transfers between devices: 4.53 us -> 20.5 us  [exchanged(): lax.all_to_all(flat, AXES, split_axis=0, concat_axis=0, tiled=True)]
    ppermute x0 -> x12, starting transfers between devices: none -> 14 us  [moved(): return lax.ppermute(value, AXES, pairs)]
  transfers between devices with their start and end apart: 3 -> 14, of which waited for: 2 -> 2; matrix products, arithmetic and copies ran while one was open for 22% -> 0% of each run, Pallas kernels for 0% -> 23%
where the time goes in v1:
time: 124 us; the launch traced here: 123 us
  Pallas kernels  43.1 us (35%)
  waiting for transfers between devices  38 us (31%)
  starting transfers between devices  34.5 us (28%)
  local copies, waits for them, and re-layouts  7.11 us (6%)
    all_to_all x2, starting transfers between devices, exchanged(): lax.all_to_all(flat, AXES, split_axis=0, concat_axis=0, tiled=True)  20.5 us
    ppermute x12, waiting for transfers between devices, moved(): return lax.ppermute(value, AXES, pairs)  20.4 us
    pallas_call x1, Pallas kernels, per_device(): call(expert_kernel, like(message, BF16), [vmem(), hbm(), hbm()], [pltpu.V...  19 us
    all_to_all x2, waiting for transfers between devices, exchanged(): lax.all_to_all(flat, AXES, split_axis=0, concat_axis=0, tiled=True)  17.6 us
    ppermute x12, starting transfers between devices, moved(): return lax.ppermute(value, AXES, pairs)  14 us
    pallas_call x1, Pallas kernels, per_device(): call(functools.partial(tail_kernel, size), like(tokens.shape, BF16), [vme...  12.1 us
    unnamed x40, local copies, waits for them, and re-layouts  7.11 us
    pallas_call x1, Pallas kernels, per_device(): call(functools.partial(relay_kernel, size), [like((4 * FAR * size, width)...  5.1 us
  transfers between devices with their start and end apart: 14, of which 2 were waited for; matrix products, arithmetic and copies ran while one was open for 0% of the time, Pallas kernels for 23%

profile of v1, /device:TPU:1, one launch (start us, length us, event | category | flops | bytes accessed | tf_op | source)
XLA Modules:
  0.0 123.2 jit_solution(1587263447559501690)
XLA Ops:
  0.0 1.1 copy-done.2
  2.5 2.5 %shard_map.112 = bf16[64,2,48,128]{3,2,1,0:T(8,128)(2,1)} custom-call(bf16[512,768]{1,0:T(8,128)(2,1)S(1)} %copy-done.2, s32[1,512]{1,0:T(1,128)S(1)} %bitcast.5, f32[768]{0:T(1024)S(1)} %copy-done.5), custom_call_target="tpu_custom_call" | custom-call | flops 805306368 | bytes 4000000 | tf_op jit(solution)/shard_map/pallas_call | solution.py:376
  5.0 11.5 %all-to-all-start = ((bf16[128,48,128]{2,1,0:T(8,128)(2,1)}), bf16[128,48,128]{2,1,0:T(8,128)(2,1)S(1)}, u32[]{:S(2)}, u32[]{:S(2)}) async-start(bf16[128,48,128]{2,1,0:T(8,128)(2,1)} %bitcast.1), calls=%async_computation | async-start | bytes 3145728 | tf_op jit(solution)/shard_map/all_to_all | solution.py:386
  16.5 2.5 %shard_map.110 = bf16[200,768]{1,0:T(8,128)(2,1)} custom-call(bf16[768,768]{1,0:T(8,128)(2,1)} %own_in.1, bf16[768,768]{1,0:T(8,128)(2,1)} %own_out.1, f32[768]{0:T(1024)} %scale_ref.3), custom_call_target="tpu_custom_call" | custom-call | bytes 600000 | tf_op jit(solution)/shard_map/pallas_call | solution.py:364
  19.0 3.3 %collective-permute-start.2 = (bf16[200,768]{1,0:T(8,128)(2,1)}, bf16[200,768]{1,0:T(8,128)(2,1)S(1)}, u32[]{:S(2)}, u32[]{:S(2)}) collective-permute-start(bf16[200,768]{1,0:T(8,128)(2,1)} %shard_map.110), channel_id=1, source_target_pairs={{0,64},{1,65},{2,66},{3,67},{4,68},{5,69},{6,70},{7,71},{8,72},{9,... | collective-permute-start | bytes 921608 | tf_op jit(solution)/shard_map/ppermute | solution.py:35
  22.9 0.8 collective-permute-start
  23.8 17.6 %all-to-all-done = bf16[128,48,128]{2,1,0:T(8,128)(2,1)S(1)} async-done(((bf16[128,48,128]{2,1,0:T(8,128)(2,1)}), bf16[128,48,128]{2,1,0:T(8,128)(2,1)S(1)}, u32[]{:S(2)}, u32[]{:S(2)}) %all-to-all-start) | async-done | bytes 1572896 | tf_op jit(solution)/shard_map/all_to_all | solution.py:386
  41.4 1.2 copy-done.11
  42.5 19.0 %shard_map.113 = bf16[64,2,48,128]{3,2,1,0:T(8,128)(2,1)} custom-call(bf16[64,2,48,128]{3,2,1,0:T(8,128)(2,1)} %bitcast.8, bf16[2,768,3072]{2,1,0:T(8,128)(2,1)} %in_hbm.3, bf16[2,3072,768]{2,1,0:T(8,128)(2,1)} %out_hbm.3), custom_call_target="tpu_custom_call" | custom-call | flops 9663676416 | bytes 20000000 | tf_op jit(solution)/shard_map/pallas_call | solution.py:415
  61.6 9.0 %all-to-all-start.1 = ((bf16[128,48,128]{2,1,0:T(8,128)(2,1)}), bf16[128,48,128]{2,1,0:T(8,128)(2,1)}, u32[]{:S(2)}, u32[]{:S(2)}) async-start(bf16[128,48,128]{2,1,0:T(8,128)(2,1)} %bitcast.7), calls=%async_computation.1 | async-start | bytes 3145728 | tf_op jit(solution)/shard_map/all_to_all | solution.py:386
  70.6 5.1 %shard_map.111 = (bf16[576,768]{1,0:T(8,128)(2,1)S(1)}, bf16[432,768]{1,0:T(8,128)(2,1)S(1)}, bf16[432,768]{1,0:T(8,128)(2,1)S(1)}, bf16[432,768]{1,0:T(8,128)(2...) custom-call(bf16[200,768]{1,0:T(8,128)(2,1)S(1)} %collective-permute-done.refs_0_, ...), custom_call_target="tpu_custom_call" | custom-call | bytes 6000000 | tf_op jit(solution)/shard_map/pallas_call | solution.py:399
  75.8 1.4 %collective-permute-start.3 = (bf16[432,768]{1,0:T(8,128)(2,1)S(1)}, bf16[432,768]{1,0:T(8,128)(2,1)S(1)}, u32[]{:S(2)}, u32[]{:S(2)}) collective-permute-start(bf16[432,768]{1,0:T(8,128)(2,1)S(1)} %get-tuple-element.17), channel_id=1, source_target_pairs={{0,2},{1,3},{2,4},{3,5},{4,6},{5,7},{6,0},{7,1},{8,10},{9,11},{10,... | collective-permute-start | bytes 1990664 | tf_op jit(solution)/shard_map/ppermute | solution.py:35
  77.2 1.3 %collective-permute-start.4 = (bf16[432,768]{1,0:T(8,128)(2,1)S(1)}, bf16[432,768]{1,0:T(8,128)(2,1)S(1)}, u32[]{:S(2)}, u32[]{:S(2)}) collective-permute-start(bf16[432,768]{1,0:T(8,128)(2,1)S(1)} %get-tuple-element.18), channel_id=1, source_target_pairs={{0,6},{1,7},{2,0},{3,1},{4,2},{5,3},{6,4},{7,5},{8,14},{9,15},{10,... | collective-permute-start | bytes 1990664 | tf_op jit(solution)/shard_map/ppermute | solution.py:35
  78.5 1.4 %collective-permute-start.5 = (bf16[432,768]{1,0:T(8,128)(2,1)S(1)}, bf16[432,768]{1,0:T(8,128)(2,1)S(1)}, u32[]{:S(2)}, u32[]{:S(2)}) collective-permute-start(bf16[432,768]{1,0:T(8,128)(2,1)S(1)} %get-tuple-element.19), channel_id=1, source_target_pairs={{0,8},{1,9},{2,10},{3,11},{4,12},{5,13},{6,14},{7,15},{8,16},{9,17... | collective-permute-start | bytes 1990664 | tf_op jit(solution)/shard_map/ppermute | solution.py:35
  79.9 1.3 %collective-permute-start.6 = (bf16[432,768]{1,0:T(8,128)(2,1)S(1)}, bf16[432,768]{1,0:T(8,128)(2,1)S(1)}, u32[]{:S(2)}, u32[]{:S(2)}) collective-permute-start(bf16[432,768]{1,0:T(8,128)(2,1)S(1)} %get-tuple-element.20), channel_id=1, source_target_pairs={{0,24},{1,25},{2,26},{3,27},{4,28},{5,29},{6,30},{7,31},{8,0},{9,1... | collective-permute-start | bytes 1990664 | tf_op jit(solution)/shard_map/ppermute | solution.py:35
  81.2 2.3 %collective-permute-start.7 = (bf16[576,768]{1,0:T(8,128)(2,1)S(1)}, bf16[576,768]{1,0:T(8,128)(2,1)S(1)}, u32[]{:S(2)}, u32[]{:S(2)}) collective-permute-start(bf16[576,768]{1,0:T(8,128)(2,1)S(1)} %get-tuple-element.16.refs_0_), channel_id=1, source_target_pairs={{0,1},{1,0},{2,3},{3,2},{4,5},{5,4},{6,7},{7,6},{8,9},{9,8},{10,11... | collective-permute-start | bytes 2654216 | tf_op jit(solution)/shard_map/ppermute | solution.py:35
  83.4 20.4 %collective-permute-done.3.refs_1_ = bf16[432,768]{1,0:T(8,128)(2,1)S(1)} collective-permute-done((bf16[432,768]{1,0:T(8,128)(2,1)S(1)}, bf16[432,768]{1,0:T(8,128)(2,1)S(1)}, u32[]{:S(2)}, u32[]{:S(2)}) %collective-permute-start.3) | collective-permute-done | bytes 663584 | tf_op jit(solution)/shard_map/ppermute | solution.py:35
  103.9 1.0 collective-permute-start.8
  105.5 1.9 %shard_map.109 = (f32[512,1]{1,0:T(8,128)S(1)}, s32[512,2]{1,0:T(8,128)S(1)}) custom-call(bf16[512,768]{1,0:T(8,128)(2,1)S(1)} %copy-done.3, s32[1,512]{1,0:T(1,128)S(1)} %bitcast.6, f32[768]{0:T(1024)S(1)} %copy-done.6, f32[768,256]{1,0:T(8,128)S(1)} %copy-done.1), custom_call_target="tpu_custom_call" | custom-call | flops 1207959552 | bytes 4000000 | tf_op jit(solution)/shard_map/pallas_call | solution.py:390
  107.4 0.7 copy-done.9
  108.1 0.7 copy-done.10
  108.9 0.9 copy-done.17
  110.0 0.8 copy-done.19
  110.9 12.1 %shard_map.114 = bf16[512,768]{1,0:T(8,128)(2,1)} custom-call(bf16[512,768]{1,0:T(8,128)(2,1)} %token_ref.5, f32[512,1]{1,0:T(8,128)} %copy-done.9, s32[512,2]{1,0:T(8,128)} %copy-done.10, f32[768]{0:T(1024)} %gain_ref.5, f32[768]{0:T(1024)} %scale_ref.3, f32[768]{0:T(1024)} %scale_out_ref.1, f32[3,1,768]{2,1,0:T(1,128)} %copy-done.4, ...), custom_call_target="tpu_custom_call" | custom-call | flops 4831838208 | bytes 12000000 | tf_op jit(solution)/shard_map/pallas_call | solution.py:432
  (50 shorter events, 2.9 us)
Async XLA Ops:
  5.0 36.3 %all-to-all-start = ((bf16[128,48,128]{2,1,0:T(8,128)(2,1)}), bf16[128,48,128]{2,1,0:T(8,128)(2,1)S(1)}, u32[]{:S(2)}, u32[]{:S(2)}) async-start(bf16[128,48,128]{2,1,0:T(8,128)(2,1)} %bitcast.1), calls=%async_computation | async-start | bytes 3145728 | tf_op jit(solution)/shard_map/all_to_all | solution.py:386
  19.0 51.6 %collective-permute-start.2 = (bf16[200,768]{1,0:T(8,128)(2,1)}, bf16[200,768]{1,0:T(8,128)(2,1)S(1)}, u32[]{:S(2)}, u32[]{:S(2)}) collective-permute-start(bf16[200,768]{1,0:T(8,128)(2,1)} %shard_map.110), channel_id=1, source_target_pairs={{0,64},{1,65},{2,66},{3,67},{4,68},{5,69},{6,70},{7,71},{8,72},{9,... | collective-permute-start | bytes 921608 | tf_op jit(solution)/shard_map/ppermute | solution.py:35
  22.3 48.3 %collective-permute-start.1 = (bf16[200,768]{1,0:T(8,128)(2,1)}, bf16[200,768]{1,0:T(8,128)(2,1)S(1)}, u32[]{:S(2)}, u32[]{:S(2)}) collective-permute-start(bf16[200,768]{1,0:T(8,128)(2,1)} %shard_map.110), channel_id=1, source_target_pairs={{0,96},{1,97},{2,98},{3,99},{4,100},{5,101},{6,102},{7,103},{8,104... | collective-permute-start | bytes 921608 | tf_op jit(solution)/shard_map/ppermute | solution.py:35
  22.9 47.7 %collective-permute-start = (bf16[200,768]{1,0:T(8,128)(2,1)}, bf16[200,768]{1,0:T(8,128)(2,1)S(1)}, u32[]{:S(2)}, u32[]{:S(2)}) collective-permute-start(bf16[200,768]{1,0:T(8,128)(2,1)} %shard_map.110), channel_id=1, source_target_pairs={{0,32},{1,33},{2,34},{3,35},{4,36},{5,37},{6,38},{7,39},{8,40},{9,... | collective-permute-start | bytes 921608 | tf_op jit(solution)/shard_map/ppermute | solution.py:35
  61.6 43.9 %copy-start.1 = (f32[768,256]{1,0:T(8,128)S(1)}, f32[768,256]{1,0:T(8,128)}, u32[]{:S(2)}) copy-start(f32[768,256]{1,0:T(8,128)} %router_ref.1) | copy-start | bytes 2359300
  61.6 43.9 %copy-start.3 = (bf16[512,768]{1,0:T(8,128)(2,1)S(1)}, bf16[512,768]{1,0:T(8,128)(2,1)}, u32[]{:S(2)}) copy-start(bf16[512,768]{1,0:T(8,128)(2,1)} %token_ref.5) | copy-start | bytes 2359300
  61.6 43.9 %copy-start.6 = (f32[768]{0:T(1024)S(1)}, f32[768]{0:T(1024)}, u32[]{:S(2)}) copy-start(f32[768]{0:T(1024)} %gain_ref.4) | copy-start | bytes 9220
  61.6 43.9 %copy-start.8 = (s32[512,1]{0,1:T(1,128)S(1)}, s32[512,1]{0,1:T(1,128)}, u32[]{:S(2)}) copy-start(s32[512,1]{0,1:T(1,128)} %param.12) | copy-start | bytes 6148
  61.6 49.3 %all-to-all-start.1 = ((bf16[128,48,128]{2,1,0:T(8,128)(2,1)}), bf16[128,48,128]{2,1,0:T(8,128)(2,1)}, u32[]{:S(2)}, u32[]{:S(2)}) async-start(bf16[128,48,128]{2,1,0:T(8,128)(2,1)} %bitcast.7), calls=%async_computation.1 | async-start | bytes 3145728 | tf_op jit(solution)/shard_map/all_to_all | solution.py:386
  75.7 31.6 %copy-start = (bf16[576,768]{1,0:T(8,128)(2,1)}, bf16[576,768]{1,0:T(8,128)(2,1)S(1)}, u32[]{:S(2)}) copy-start(bf16[576,768]{1,0:T(8,128)(2,1)S(1)} %get-tuple-element.16.refs_0_) | copy-start | bytes 2654212
  75.8 31.6 %copy-start.4 = (f32[3,1,768]{2,1,0:T(1,128)}, f32[3,1,768]{2,1,0:T(1,128)S(1)}, u32[]{:S(2)}) copy-start(f32[3,1,768]{2,1,0:T(1,128)S(1)} %get-tuple-element.15.far_scale_ref) | copy-start | bytes 27652
  75.8 28.1 %collective-permute-start.3 = (bf16[432,768]{1,0:T(8,128)(2,1)S(1)}, bf16[432,768]{1,0:T(8,128)(2,1)S(1)}, u32[]{:S(2)}, u32[]{:S(2)}) collective-permute-start(bf16[432,768]{1,0:T(8,128)(2,1)S(1)} %get-tuple-element.17), channel_id=1, source_target_pairs={{0,2},{1,3},{2,4},{3,5},{4,6},{5,7},{6,0},{7,1},{8,10},{9,11},{10,... | collective-permute-start | bytes 1990664 | tf_op jit(solution)/shard_map/ppermute | solution.py:35
  77.2 27.6 %collective-permute-start.4 = (bf16[432,768]{1,0:T(8,128)(2,1)S(1)}, bf16[432,768]{1,0:T(8,128)(2,1)S(1)}, u32[]{:S(2)}, u32[]{:S(2)}) collective-permute-start(bf16[432,768]{1,0:T(8,128)(2,1)S(1)} %get-tuple-element.18), channel_id=1, source_target_pairs={{0,6},{1,7},{2,0},{3,1},{4,2},{5,3},{6,4},{7,5},{8,14},{9,15},{10,... | collective-permute-start | bytes 1990664 | tf_op jit(solution)/shard_map/ppermute | solution.py:35
  78.5 26.4 %collective-permute-start.5 = (bf16[432,768]{1,0:T(8,128)(2,1)S(1)}, bf16[432,768]{1,0:T(8,128)(2,1)S(1)}, u32[]{:S(2)}, u32[]{:S(2)}) collective-permute-start(bf16[432,768]{1,0:T(8,128)(2,1)S(1)} %get-tuple-element.19), channel_id=1, source_target_pairs={{0,8},{1,9},{2,10},{3,11},{4,12},{5,13},{6,14},{7,15},{8,16},{9,17... | collective-permute-start | bytes 1990664 | tf_op jit(solution)/shard_map/ppermute | solution.py:35
  79.9 25.5 %collective-permute-start.6 = (bf16[432,768]{1,0:T(8,128)(2,1)S(1)}, bf16[432,768]{1,0:T(8,128)(2,1)S(1)}, u32[]{:S(2)}, u32[]{:S(2)}) collective-permute-start(bf16[432,768]{1,0:T(8,128)(2,1)S(1)} %get-tuple-element.20), channel_id=1, source_target_pairs={{0,24},{1,25},{2,26},{3,27},{4,28},{5,29},{6,30},{7,31},{8,0},{9,1... | collective-permute-start | bytes 1990664 | tf_op jit(solution)/shard_map/ppermute | solution.py:35
  81.2 27.6 %collective-permute-start.7 = (bf16[576,768]{1,0:T(8,128)(2,1)S(1)}, bf16[576,768]{1,0:T(8,128)(2,1)S(1)}, u32[]{:S(2)}, u32[]{:S(2)}) collective-permute-start(bf16[576,768]{1,0:T(8,128)(2,1)S(1)} %get-tuple-element.16.refs_0_), channel_id=1, source_target_pairs={{0,1},{1,0},{2,3},{3,2},{4,5},{5,4},{6,7},{7,6},{8,9},{9,8},{10,11... | collective-permute-start | bytes 2654216 | tf_op jit(solution)/shard_map/ppermute | solution.py:35
  103.9 3.5 %copy-start.13 = (bf16[432,768]{1,0:T(8,128)(2,1)}, bf16[432,768]{1,0:T(8,128)(2,1)S(1)}, u32[]{:S(2)}) copy-start(bf16[432,768]{1,0:T(8,128)(2,1)S(1)} %collective-permute-done.3.refs_1_) | copy-start | bytes 1990660
  103.9 5.0 %collective-permute-start.8 = (bf16[432,768]{1,0:T(8,128)(2,1)S(1)}, bf16[432,768]{1,0:T(8,128)(2,1)S(1)}, u32[]{:S(2)}, u32[]{:S(2)}) collective-permute-start(bf16[432,768]{1,0:T(8,128)(2,1)S(1)} %collective-permute-done.3.refs_1_), channel_id=1, source_target_pairs={{0,1},{1,0},{2,3},{3,2},{4,5},{5,4},{6,7},{7,6},{8,9},{9,8},{10,11... | collective-permute-start | bytes 1990664 | tf_op jit(solution)/shard_map/ppermute | solution.py:35
  104.8 2.6 %copy-start.14 = (bf16[432,768]{1,0:T(8,128)(2,1)}, bf16[432,768]{1,0:T(8,128)(2,1)S(1)}, u32[]{:S(2)}) copy-start(bf16[432,768]{1,0:T(8,128)(2,1)S(1)} %collective-permute-done.4.refs_2_) | copy-start | bytes 1990660
  104.8 4.0 %collective-permute-start.9 = (bf16[432,768]{1,0:T(8,128)(2,1)S(1)}, bf16[432,768]{1,0:T(8,128)(2,1)S(1)}, u32[]{:S(2)}, u32[]{:S(2)}) collective-permute-start(bf16[432,768]{1,0:T(8,128)(2,1)S(1)} %collective-permute-done.4.refs_2_), channel_id=1, source_target_pairs={{0,1},{1,0},{2,3},{3,2},{4,5},{5,4},{6,7},{7,6},{8,9},{9,8},{10,11... | collective-permute-start | bytes 1990664 | tf_op jit(solution)/shard_map/ppermute | solution.py:35
  104.9 2.5 %copy-start.15 = (bf16[432,768]{1,0:T(8,128)(2,1)}, bf16[432,768]{1,0:T(8,128)(2,1)S(1)}, u32[]{:S(2)}) copy-start(bf16[432,768]{1,0:T(8,128)(2,1)S(1)} %collective-permute-done.5.refs_3_) | copy-start | bytes 1990660
  104.9 3.9 %collective-permute-start.10 = (bf16[432,768]{1,0:T(8,128)(2,1)S(1)}, bf16[432,768]{1,0:T(8,128)(2,1)S(1)}, u32[]{:S(2)}, u32[]{:S(2)}) collective-permute-start(bf16[432,768]{1,0:T(8,128)(2,1)S(1)} %collective-permute-done.5.refs_3_), channel_id=1, source_target_pairs={{0,1},{1,0},{2,3},{3,2},{4,5},{5,4},{6,7},{7,6},{8,9},{9,8},{10,11... | collective-permute-start | bytes 1990664 | tf_op jit(solution)/shard_map/ppermute | solution.py:35
  105.4 5.5 %collective-permute-start.11 = (bf16[432,768]{1,0:T(8,128)(2,1)S(1)}, bf16[432,768]{1,0:T(8,128)(2,1)}, u32[]{:S(2)}, u32[]{:S(2)}) collective-permute-start(bf16[432,768]{1,0:T(8,128)(2,1)S(1)} %collective-permute-done.6.refs_4_), channel_id=1, source_target_pairs={{0,1},{1,0},{2,3},{3,2},{4,5},{5,4},{6,7},{7,6},{8,9},{9,8},{10,11... | collective-permute-start | bytes 1990664 | tf_op jit(solution)/shard_map/ppermute | solution.py:35
  108.8 2.0 %copy-start.12 = (bf16[576,768]{1,0:T(8,128)(2,1)}, bf16[576,768]{1,0:T(8,128)(2,1)S(1)}, u32[]{:S(2)}) copy-start(bf16[576,768]{1,0:T(8,128)(2,1)S(1)} %collective-permute-done.7.refs_5_) | copy-start | bytes 2654212
  (10 other events, 10.1 us)
